TPU v7x, 32 devices: a whole 2x2x4 slice. The times are simulated.
32 devices in a mesh: body: 4 (over y, core), surf: 8 (over z, x).
Axes of the slice: x: 2, y: 2, z: 4, core: 2. Of those that a mesh axis runs over, the one named last changes fastest.
Arguments:
- external_load: float32 [3, 32, 128, 1024], P(None, 'body', 'surf'), may hold values from -18 to 18
- modulus: float32 [32, 128, 1024], P('body', 'surf'), may hold values from 0.2 to 10, as said below
- active: int32 [128, 1024], P('surf'), may hold values 0 or 1
Outputs:
- lam_depth: float32 [3, 4, 128, 1024], P(None, 'body', 'surf')
- lam_surface: float32 [3, 32, 8, 1024], P(None, 'body', 'surf')
- lam_contact: float32 [4, 128, 1024], P('body', 'surf')
Inputs may be any that keep to these rules, and one draw needn't show every extreme that they name: The modulus is positive.
All inputs are finite; a program needn't handle non-finite values. No bound on the sum of `active` on one device may be relied on, other than what follows from the above.
Results may differ from a plain program's by a relative error of at most 0.0003.
Values sent between devices are 32-bit elements; how exact they have to be, the bound alone decides.
A program may use at most 192 MiB of HBM per device.

v0:
```python
import functools

import jax
import jax.numpy as jnp
import numpy as np
from jax import lax
from jax.experimental import pallas as pl
from jax.experimental.pallas import tpu as pltpu
from jax.sharding import PartitionSpec as P

ITERS = 3
SWEEPS = 6
COUPLING_SCALE = (0.0, 1.0, 0.5, 0.25)
RELAXATION = 0.6
PLANE = [(dx, dy) for dx in (-1, 0, 1) for dy in (-1, 0, 1)]
SAME = [o for o in PLANE if o != (0, 0)]
SUB, LANE = 8, 128


def shift_up(t):
    lane = lax.broadcasted_iota(jnp.int32, t.shape, 1)
    r = pltpu.roll(t, 1, 1)
    return jnp.where(lane == 0, pltpu.roll(r, 1, 0), r)


def shift_down(t):
    lane = lax.broadcasted_iota(jnp.int32, t.shape, 1)
    r = pltpu.roll(t, LANE - 1, 1)
    return jnp.where(lane == LANE - 1, pltpu.roll(r, SUB - 1, 0), r)


def setup_weights(nx, ny, mod_ref, mp, w_ref, q_ref):
    zero = jnp.zeros((SUB, LANE), jnp.float32)

    def clear(y, c):
        mp[0, y] = zero
        mp[nx + 1, y] = zero
        return c

    lax.fori_loop(0, ny + 2, clear, 0)

    def fill(x, c):
        mp[x + 1, 0] = zero
        mp[x + 1, ny + 1] = zero
        mp[x + 1, pl.ds(1, ny)] = mod_ref[x]
        return c

    lax.fori_loop(0, nx, fill, 0)
    sub = lax.broadcasted_iota(jnp.int32, (SUB, LANE), 0)
    lane = lax.broadcasted_iota(jnp.int32, (SUB, LANE), 1)
    first = (sub == 0) & (lane == 0)
    last = (sub == SUB - 1) & (lane == LANE - 1)

    def column(i, c):
        x = i // ny
        y = i % ny
        a = mp[x + 1, y + 1]
        up = jnp.where(first, 0.0, shift_up(a))
        down = jnp.where(last, 0.0, shift_down(a))
        total0 = zero
        total_p = zero
        total_m = zero
        for dx, dy in PLANE:
            b = mp[x + 1 + dx, y + 1 + dy]
            k = abs(dx) + abs(dy)
            if k:
                w = (2.0 * COUPLING_SCALE[k]) * a * b / (a + b)
                w_ref[SAME.index((dx, dy)), x, y] = w
                total0 = total0 + w
            scale = 2.0 * COUPLING_SCALE[k + 1]
            j = PLANE.index((dx, dy))
            w = scale * up * b / jnp.maximum(up + b, 1e-30)
            w_ref[8 + j, x, y] = w
            total_p = total_p + w
            w = scale * down * b / jnp.maximum(down + b, 1e-30)
            w_ref[17 + j, x, y] = w
            total_m = total_m + w
        diag = total0 + shift_down(total_p) + shift_up(total_m)
        q_ref[x, y] = RELAXATION / diag
        return c

    lax.fori_loop(0, nx * ny, column, 0)


def column_update(x, y, src, dst, s_ref, w_ref, q_ref):
    center, plus, minus, mid = [], [], [], []
    for comp in range(3):
        mid.append(s_ref[comp, x, y])
    for n, (dx, dy) in enumerate(PLANE):
        wp = w_ref[8 + n, x, y]
        wm = w_ref[17 + n, x, y]
        w0 = w_ref[SAME.index((dx, dy)), x, y] if (dx, dy) != (0, 0) else None
        for comp in range(3):
            v = src[comp, x + 1 + dx, y + 1 + dy]
            if n == 0:
                plus.append(wp * v)
                minus.append(wm * v)
            else:
                plus[comp] = plus[comp] + wp * v
                minus[comp] = minus[comp] + wm * v
            if w0 is None:
                center.append(v)
            else:
                mid[comp] = mid[comp] + w0 * v
    q = q_ref[x, y]
    for comp in range(3):
        total = mid[comp] + shift_down(plus[comp]) + shift_up(minus[comp])
        dst[comp, x + 1, y + 1] = (1.0 - RELAXATION) * center[comp] + q * total


def sweep(nx, ny, depth, src, dst, s_ref, w_ref, q_ref):
    full = min(nx, 2 * (depth + 1))
    step = 4

    def rows(i, c):
        r = i // (ny // step)
        y0 = (i % (ny // step)) * step
        x = r if full == nx else jnp.where(r <= depth, r, r + (nx - full))
        for j in range(step):
            column_update(x, y0 + j, src, dst, s_ref, w_ref, q_ref)
        return c

    lax.fori_loop(0, full * (ny // step), rows, 0)
    if full < nx:
        def sides(i, c):
            x = depth + 1 + i
            for j in range(depth + 1):
                column_update(x, j, src, dst, s_ref, w_ref, q_ref)
                column_update(x, ny - 1 - j, src, dst, s_ref, w_ref, q_ref)
            return c

        lax.fori_loop(0, nx - full, sides, 0)


def relax(nx, ny, local, va, vb, s_ref, w_ref, q_ref):
    deepest = (min(nx, ny) - 1) // 2

    def start(x, c):
        for comp in range(3):
            va[comp, x + 1, pl.ds(1, ny)] = q_ref[x] * s_ref[comp, x]
            if local:
                vb[comp, x + 1, pl.ds(1, ny)] = jnp.zeros((ny, SUB, LANE), jnp.float32)
        return c

    lax.fori_loop(0, nx, start, 0)
    bufs = (va, vb)
    for k in range(1, SWEEPS):
        depth = min(deepest, SWEEPS - 1 - k)
        if local:
            depth = min(depth, k)
        sweep(nx, ny, depth, bufs[(k - 1) % 2], bufs[k % 2], s_ref, w_ref, q_ref)
    return bufs[(SWEEPS - 1) % 2]


def clear_halo(nx, ny, va, vb):
    zero = jnp.zeros((SUB, LANE), jnp.float32)
    for v in (va, vb):
        for comp in range(3):
            v[comp, 0] = jnp.zeros((ny + 2, SUB, LANE), jnp.float32)
            v[comp, nx + 1] = jnp.zeros((ny + 2, SUB, LANE), jnp.float32)

            def side(x, c):
                v[comp, x + 1, 0] = zero
                v[comp, x + 1, ny + 1] = zero
                return c

            lax.fori_loop(0, nx, side, 0)


def add_faces(nx, ny, s_ref, own_x, up_x, own_y, left_y, contact, mask, sign):
    for comp in range(3):
        s_ref[comp, nx - 1] = s_ref[comp, nx - 1] + sign * own_x[comp]
        s_ref[comp, 0] = s_ref[comp, 0] - sign * up_x[comp]

        def side(x, c):
            s_ref[comp, x, ny - 1] = s_ref[comp, x, ny - 1] + sign * own_y[comp, x]
            s_ref[comp, x, 0] = s_ref[comp, x, 0] - sign * left_y[comp, x]
            return c

        lax.fori_loop(0, nx, side, 0)
    s_ref[0, 0] = s_ref[0, 0] - sign * contact[...] * mask[...]


def take_faces(nx, ny, v, first_x, last_x, first_y, last_y):
    for comp in range(3):
        first_x[comp] = v[comp, 1, pl.ds(1, ny)]
        last_x[comp] = v[comp, nx, pl.ds(1, ny)]

        def side(x, c):
            first_y[comp, x] = v[comp, x + 1, 1]
            last_y[comp, x] = v[comp, x + 1, ny]
            return c

        lax.fori_loop(0, nx, side, 0)


def load_kernel(nx, ny, load, mod, own_x, up_x, own_y, left_y, contact, mask,
                w_ref, q_ref, first_x, last_x, first_y, last_y, mp, va, vb, s_ref):
    setup_weights(nx, ny, mod, mp, w_ref, q_ref)
    clear_halo(nx, ny, va, vb)
    s_ref[...] = load[...]
    add_faces(nx, ny, s_ref, own_x, up_x, own_y, left_y, contact, mask, -1.0)
    v = relax(nx, ny, False, va, vb, s_ref, w_ref, q_ref)
    take_faces(nx, ny, v, first_x, last_x, first_y, last_y)


def direction_kernel(nx, ny, w_ref, q_ref, own_x, up_x, own_y, left_y, contact, mask,
                     first_x, last_x, first_y, last_y, va, vb, s_ref):
    clear_halo(nx, ny, va, vb)
    s_ref[...] = jnp.zeros_like(s_ref)
    add_faces(nx, ny, s_ref, own_x, up_x, own_y, left_y, contact, mask, 1.0)
    v = relax(nx, ny, True, va, vb, s_ref, w_ref, q_ref)
    take_faces(nx, ny, v, first_x, last_x, first_y, last_y)


def coarse_constants(n_depth, n_across, face_x, face_y):
    path = 2.0 * np.eye(n_depth) - np.eye(n_depth, k=1) - np.eye(n_depth, k=-1)
    path[0, 0] = 1.0
    eye = np.eye(n_across)
    cycle = 2.0 * eye - np.roll(eye, 1, axis=1) - np.roll(eye, -1, axis=1)
    base = face_x * np.kron(path, eye) + face_y * np.kron(np.eye(n_depth), cycle)
    return np.linalg.inv(base)


def vmem(count):
    return [pl.BlockSpec(memory_space=pltpu.VMEM)] * count


def shards(external_load, modulus, active):
    nx, ny, nz = modulus.shape
    depth_index = lax.axis_index("body")
    across_index = lax.axis_index("surf")
    n_depth = lax.axis_size("body")
    n_across = lax.axis_size("surf")
    total = n_depth * n_across
    own_index = depth_index * n_across + across_index
    inner = (depth_index > 0).astype(jnp.float32)
    mask = active.astype(jnp.float32) * (1.0 - inner)
    f32 = jnp.float32
    hi = lax.Precision.HIGHEST
    inverse = coarse_constants(n_depth, n_across, float(ny * nz), float(nx * nz))
    inv = jnp.asarray(inverse, f32)
    load = external_load.reshape(3, nx, ny, SUB, LANE)
    mod = modulus.reshape(nx, ny, SUB, LANE)
    mask = mask.reshape(ny, SUB, LANE)

    sums = jnp.concatenate([jnp.sum(load, axis=(1, 2, 3, 4)), jnp.sum(mask)[None]])
    gathered = lax.all_gather(sums[None], ("body", "surf"), axis=0, tiled=True)
    counts = gathered[:, 3]
    root = jnp.sqrt(counts[:n_across])
    small = jnp.eye(n_across, dtype=f32) + root[:, None] * inv[:n_across, :n_across] * root[None, :]
    work = jnp.concatenate([small, jnp.eye(n_across, dtype=f32)], 1)
    for k in range(n_across):
        pivot = work[k] / work[k, k]
        work = (work - work[:, k : k + 1] * pivot[None]).at[k].set(pivot)
    left = inv[:, :n_across] * root[None, :]
    normal = inv - jnp.dot(left, jnp.dot(work[:, n_across:], left.T, precision=hi), precision=hi)

    def coarse_solve(rhs):
        a = jnp.dot(normal, rhs[:, 0:1], precision=hi)
        b = jnp.dot(inv, rhs[:, 1:3], precision=hi)
        return jnp.concatenate([a, b], 1)

    def constants(alpha):
        grid = alpha.reshape(n_depth, n_across, 3)
        below = jnp.concatenate([grid[1:], jnp.zeros((1, n_across, 3), f32)], 0)
        along_x = grid - below
        along_y = grid - jnp.roll(grid, -1, axis=1)
        return along_x, along_y

    def lift(alpha):
        along_x, along_y = constants(alpha)
        zero_row = jnp.zeros((1, n_across, 3), f32)
        above = jnp.concatenate([zero_row, along_x[:-1]], 0)
        lefts = jnp.roll(along_y, 1, axis=1)
        table = jnp.concatenate([along_x, above, along_y, lefts, alpha.reshape(n_depth, n_across, 3)], 2)
        mine = lax.dynamic_slice_in_dim(table.reshape(total, 15), own_index, 1, 0)[0]

        def wide(c, n):
            return jnp.broadcast_to(c[:, None, None, None], (3, n, SUB, LANE))

        return (wide(mine[0:3], ny), wide(mine[3:6], ny), wide(mine[6:9], nx),
                wide(mine[9:12], nx), -mine[12] * mask)

    own_count = jnp.sum(mask)

    def statistics(v):
        sx = jnp.sum(v[0], axis=(1, 2, 3))
        sy = jnp.sum(v[2], axis=(1, 2, 3))
        sc = jnp.sum(v[4])
        cx = v[0] - (sx / (ny * nz))[:, None, None, None]
        cy = v[2] - (sy / (nx * nz))[:, None, None, None]
        cc = v[4] - sc / jnp.maximum(own_count, 1.0) * mask
        ss = jnp.sum(cx * cx) + jnp.sum(cy * cy) + jnp.sum(cc * cc)
        return jnp.concatenate([sx, sy, sc[None], ss[None]])

    def own_dot(a, b):
        return jnp.sum(a[0] * b[0]) + jnp.sum(a[2] * b[2]) + jnp.sum(a[4] * b[4])

    def projection(table):
        sx = table[:, 0:3].reshape(n_depth, n_across, 3)
        sy = table[:, 3:6].reshape(n_depth, n_across, 3)
        sc = table[:, 6]
        above = jnp.concatenate([jnp.zeros((1, n_across, 3), f32), sx[:-1]], 0)
        rhs = (sx - above + sy - jnp.roll(sy, 1, axis=1)).reshape(total, 3)
        rhs = rhs.at[:, 0].add(-sc)
        alpha = coarse_solve(rhs)
        along_x, along_y = constants(alpha)
        ex = sx / (ny * nz) - along_x
        ey = sy / (nx * nz) - along_y
        ec = sc / jnp.maximum(counts, 1.0) + alpha[:, 0]
        norm = (jnp.sum(table[:, 7]) + (ny * nz) * jnp.sum(ex * ex)
                + (nx * nz) * jnp.sum(ey * ey) + jnp.sum(counts * ec * ec))
        return alpha, norm

    def axpy(a, b, s):
        return tuple(x + s * y for x, y in zip(a, b))

    def gather(values):
        return lax.all_gather(values[None], ("body", "surf"), axis=0, tiled=True)

    x_shape = jax.ShapeDtypeStruct((3, ny, SUB, LANE), f32)
    y_shape = jax.ShapeDtypeStruct((3, nx, SUB, LANE), f32)
    faces = (x_shape, x_shape, y_shape, y_shape)
    iterate = pltpu.VMEM((3, nx + 2, ny + 2, SUB, LANE), f32)
    source = pltpu.VMEM((3, nx, ny, SUB, LANE), f32)
    params = pltpu.CompilerParams(vmem_limit_bytes=56 * 1024 * 1024)
    first_call = pl.pallas_call(
        functools.partial(load_kernel, nx, ny),
        out_shape=(jax.ShapeDtypeStruct((26, nx, ny, SUB, LANE), f32),
                   jax.ShapeDtypeStruct((nx, ny, SUB, LANE), f32)) + faces,
        in_specs=vmem(8), out_specs=tuple(vmem(6)),
        scratch_shapes=[pltpu.VMEM((nx + 2, ny + 2, SUB, LANE), f32), iterate, iterate, source],
        compiler_params=params,
    )
    later_call = pl.pallas_call(
        functools.partial(direction_kernel, nx, ny),
        out_shape=faces, in_specs=vmem(8), out_specs=tuple(vmem(4)),
        scratch_shapes=[iterate, iterate, source],
        compiler_params=params,
    )

    def jumps(first_x, last_x, first_y, last_y):
        pairs = [(b, b + 1) for b in range(n_depth - 1)]
        ring = [(b, (b + 1) % n_across) for b in range(n_across)]
        back = lambda p: [(t, s) for s, t in p]
        from_above = lax.ppermute(last_x, "body", pairs)
        from_below = lax.ppermute(first_x, "body", back(pairs))
        from_left = lax.ppermute(last_y, "surf", ring)
        from_right = lax.ppermute(first_y, "surf", back(ring))
        return (last_x - from_below, inner * (from_above - first_x), last_y - from_right,
                from_left - first_y, -first_x[0] * mask)

    multipliers = lift(coarse_solve(gathered[:, 0:3]))
    outs = first_call(load, mod, *multipliers, mask)
    weights, q = outs[0], outs[1]
    gradient = tuple(-piece for piece in jumps(*outs[2:]))
    alpha, rr = projection(gather(statistics(gradient)))
    residual = axpy(gradient, lift(alpha), -1.0)
    direction = residual
    for step_index in range(ITERS):
        f = later_call(weights, q, *direction, mask)
        local = (jnp.sum(direction[0] * f[1]) - jnp.sum(direction[1] * f[0])
                 + jnp.sum(direction[2] * f[3]) - jnp.sum(direction[3] * f[2])
                 - jnp.sum(direction[4] * f[0][0] * mask))
        if step_index + 1 == ITERS:
            bottom = jnp.sum(gather(local[None]))
            multipliers = axpy(multipliers, direction, rr / bottom)
            break
        image = jumps(*f)
        table = gather(jnp.concatenate(
            [statistics(image), local[None], own_dot(residual, image)[None]]))
        step = rr / jnp.sum(table[:, 8])
        alpha, ii = projection(table)
        new = rr + 2.0 * step * jnp.sum(table[:, 9]) + step * step * ii
        multipliers = axpy(multipliers, direction, step)
        residual = axpy(residual, axpy(image, lift(alpha), -1.0), step)
        direction = axpy(residual, direction, new / rr)
        rr = new
    return (multipliers[0].reshape(3, 1, ny, nz), multipliers[2].reshape(3, nx, 1, nz),
            multipliers[4].reshape(1, ny, nz))


def solution(mesh):
    placed = (P(None, "body", "surf", None), P("body", "surf", None), P("surf", None))
    return jax.shard_map(
        shards,
        mesh=mesh,
        in_specs=placed,
        out_specs=(
            P(None, "body", "surf", None),
            P(None, "body", "surf", None),
            P("body", "surf", None),
        ),
        check_vma=False,
    )
```

profile of v0, /device:TPU:0, one launch (start us, length us, event | category | flops | bytes accessed | tf_op | source)
XLA Modules:
  0.0 474.9 jit_solution(7839288143039809803)
XLA Ops:
  0.7 1.7 fusion.26
  2.4 1.7 reduce_sum.526
  4.9 42.0 %all-reduce.11 = f32[128]{0:T(128)S(1)} all-reduce(f32[128]{0:T(128)S(1)} %maximum_dynamic-update-slice_fusion), channel_id=2, replica_groups=mesh['body'=4,'surf'=8] {'body','surf'}, use_global_device_ids=true, to_apply=%add.11 | all-reduce | flops 128 | bytes 1024
  74.3 47.6 %shard_map.67 = (f32[26,8,16,8,128]{4,3,2,1,0:T(8,128)}, f32[8,16,8,128]{3,2,1,0:T(8,128)}, f32[3,16,8,128]{3,2,1,0:T(8,128)}, f32[3,16,8,128]{3,2,1,0:T(8,128)}...) custom-call(f32[3,8,16,8,128]{4,3,2,1,0:T(8,128)} %bitcast.288, f32[8,16,8,128]{3,2,1,0:T(8,128)} %bitcast.304, ...), custom_call_target="tpu_custom_call" | custom-call | tf_op jit(solution)/shard_map/pallas_call | solution.py:355
  121.9 4.0 collective-permute-start.1
  127.2 3.0 collective-permute-start.2
  138.2 1.7 multiply_reduce_fusion.10
  142.0 38.8 %all-reduce.12 = f32[256]{0:T(256)S(1)} all-reduce(f32[256]{0:T(256)S(1)} %maximum_dynamic-update-slice_fusion.1), channel_id=3, replica_groups=mesh['body'=4,'surf'=8] {'body','surf'}, use_global_device_ids=true, to_apply=%add.12 | all-reduce | flops 256 | bytes 2048
  190.7 22.4 %shard_map.68 = (f32[3,16,8,128]{3,2,1,0:T(8,128)}, f32[3,16,8,128]{3,2,1,0:T(8,128)}, f32[3,8,8,128]{3,2,1,0:T(8,128)}, f32[3,8,8,128]{3,2,1,0:T(8,128)}) custom-call(f32[26,8,16,8,128]{4,3,2,1,0:T(8,128)} %get-tuple-element.157.w_ref, f32[8,16,8,128]{3,2,1,0:T(8,128)} %get-tuple-element.158.q_ref, f32[3,16,8,128]{3,2,1,0:T(8,128)} %negate_add_fusion.1.own_x, ...), custom_call_target="tpu_custom_call" | custom-call | tf_op jit(solution)/shard_map/pallas_call | solution.py:362
  215.3 4.0 collective-permute-start.5
  219.3 1.6 multiply_reduce_fusion.18
  220.9 1.7 multiply_reduce_fusion.7
  224.0 2.8 collective-permute-start.6
  230.3 1.7 multiply_reduce_fusion.17
  240.7 40.7 %all-reduce.13 = f32[320]{0:T(512)S(1)} all-reduce(f32[320]{0:T(512)S(1)} %dynamic-update-slice.35), channel_id=4, replica_groups=mesh['body'=4,'surf'=8] {'body','surf'}, use_global_device_ids=true, to_apply=%add.13 | all-reduce | flops 320 | bytes 2560
  296.7 22.4 %shard_map.69 = (f32[3,16,8,128]{3,2,1,0:T(8,128)}, f32[3,16,8,128]{3,2,1,0:T(8,128)}, f32[3,8,8,128]{3,2,1,0:T(8,128)}, f32[3,8,8,128]{3,2,1,0:T(8,128)}) custom-call(f32[26,8,16,8,128]{4,3,2,1,0:T(8,128)} %get-tuple-element.157.w_ref, f32[8,16,8,128]{3,2,1,0:T(8,128)} %get-tuple-element.158.q_ref, f32[3,16,8,128]{3,2,1,0:T(8,128)} %multiply_add_fusion.5.own_x, ...), custom_call_target="tpu_custom_call" | custom-call | tf_op jit(solution)/shard_map/pallas_call | solution.py:362
  322.9 3.9 collective-permute-start.9
  329.0 2.7 collective-permute-start.10
  333.3 1.6 fusion.70
  344.8 39.0 %all-reduce.14 = f32[320]{0:T(512)S(1)} all-reduce(f32[320]{0:T(512)S(1)} %dynamic-update-slice.36), channel_id=5, replica_groups=mesh['body'=4,'surf'=8] {'body','surf'}, use_global_device_ids=true, to_apply=%add.14 | all-reduce | flops 320 | bytes 2560
  396.3 1.6 multiply_add_fusion.8.left_y
  399.5 22.4 %shard_map.70 = (f32[3,16,8,128]{3,2,1,0:T(8,128)}, f32[3,16,8,128]{3,2,1,0:T(8,128)}, f32[3,8,8,128]{3,2,1,0:T(8,128)}, f32[3,8,8,128]{3,2,1,0:T(8,128)}) custom-call(f32[26,8,16,8,128]{4,3,2,1,0:T(8,128)} %get-tuple-element.157.w_ref, f32[8,16,8,128]{3,2,1,0:T(8,128)} %get-tuple-element.158.q_ref, f32[3,16,8,128]{3,2,1,0:T(8,128)} %multiply_add_fusion.2.own_x, ...), custom_call_target="tpu_custom_call" | custom-call | tf_op jit(solution)/shard_map/pallas_call | solution.py:362
  423.4 1.7 multiply_reduce_fusion
  430.0 41.4 %all-reduce.15 = f32[32]{0:T(128)S(1)} all-reduce(f32[32]{0:T(128)S(1)} %dynamic-update-slice.37), channel_id=1, replica_groups=mesh['body'=4,'surf'=8] {'body','surf'}, use_global_device_ids=true, to_apply=%add.15 | all-reduce | flops 32 | bytes 256
  (336 shorter events, 86.8 us)
Async XLA Ops:
  0.6 64.1 %copy-start.27 = (f32[32,32]{1,0:T(8,128)S(1)}, f32[32,32]{1,0:T(8,128)}, u32[]{:S(2)}) copy-start(f32[32,32]{1,0:T(8,128)} %constant.340.clone) | copy-start | bytes 12292
  0.7 64.5 %copy-start.31 = (f32[32,8]{1,0:T(8,128)S(1)}, f32[32,8]{1,0:T(8,128)}, u32[]{:S(2)}) copy-start(f32[32,8]{1,0:T(8,128)} %constant.363) | copy-start | bytes 3076
  0.7 67.4 %copy-start.1 = (f32[3,8,16,1024]{3,2,1,0:T(8,128)S(1)}, f32[3,8,16,1024]{3,2,1,0:T(8,128)}, u32[]{:S(2)}) copy-start(f32[3,8,16,1024]{3,2,1,0:T(8,128)} %param.26) | copy-start | bytes 4718596
  121.9 63.9 %copy-start.16 = (f32[3,16,8,128]{3,2,1,0:T(8,128)S(1)}, f32[3,16,8,128]{3,2,1,0:T(8,128)}, u32[]{:S(2)}) copy-start(f32[3,16,8,128]{3,2,1,0:T(8,128)} %get-tuple-element.153) | copy-start | bytes 589828
  121.9 64.7 %copy-start.23 = (f32[3,8,8,128]{3,2,1,0:T(8,128)S(1)}, f32[3,8,8,128]{3,2,1,0:T(8,128)}, u32[]{:S(2)}) copy-start(f32[3,8,8,128]{3,2,1,0:T(8,128)} %get-tuple-element.155) | copy-start | bytes 294916
  121.9 66.6 %copy-start.30 = (f32[3,8,8,128]{3,2,1,0:T(8,128)S(1)}, f32[3,8,8,128]{3,2,1,0:T(8,128)}, u32[]{:S(2)}) copy-start(f32[3,8,8,128]{3,2,1,0:T(8,128)} %get-tuple-element.156) | copy-start | bytes 294916
  121.9 12.6 %collective-permute-start.1 = (f32[3,8,8,128]{3,2,1,0:T(8,128)}, f32[3,8,8,128]{3,2,1,0:T(8,128)S(1)}, u32[]{:S(2)}, u32[]{:S(2)}) collective-permute-start(f32[3,8,8,128]{3,2,1,0:T(8,128)} %get-tuple-element.156), channel_id=1, source_target_pairs={{1,0},{2,1},{3,2},{4,3},{5,4},{6,5},{7,6},{0,7},{9,8},{10,9},{11,1... | collective-permute-start | bytes 294920 | tf_op jit(solution)/shard_map/ppermute | solution.py:350
  125.9 11.3 %collective-permute-start = (f32[3,16,8,128]{3,2,1,0:T(8,128)}, f32[3,16,8,128]{3,2,1,0:T(8,128)S(1)}, u32[]{:S(2)}, u32[]{:S(2)}) collective-permute-start(f32[3,16,8,128]{3,2,1,0:T(8,128)} %get-tuple-element.154), channel_id=1, source_target_pairs={{8,0},{16,8},{24,16},{9,1},{17,9},{25,17},{10,2},{18,10},{26,18},{... | collective-permute-start | bytes 589832 | tf_op jit(solution)/shard_map/ppermute | solution.py:348
  127.2 61.4 %collective-permute-start.3 = (f32[3,8,8,128]{3,2,1,0:T(8,128)}, f32[3,8,8,128]{3,2,1,0:T(8,128)S(1)}, u32[]{:S(2)}, u32[]{:S(2)}) collective-permute-start(f32[3,8,8,128]{3,2,1,0:T(8,128)} %get-tuple-element.155), channel_id=1, source_target_pairs={{0,1},{1,2},{2,3},{3,4},{4,5},{5,6},{6,7},{7,0},{8,9},{9,10},{10,1... | collective-permute-start | bytes 294920 | tf_op jit(solution)/shard_map/ppermute | solution.py:349
  127.2 62.7 %collective-permute-start.2 = (f32[3,16,8,128]{3,2,1,0:T(8,128)}, f32[3,16,8,128]{3,2,1,0:T(8,128)S(1)}, u32[]{:S(2)}, u32[]{:S(2)}) collective-permute-start(f32[3,16,8,128]{3,2,1,0:T(8,128)} %get-tuple-element.153), channel_id=1, source_target_pairs={{0,8},{8,16},{16,24},{1,9},{9,17},{17,25},{2,10},{10,18},{18,26},{... | collective-permute-start | bytes 589832 | tf_op jit(solution)/shard_map/ppermute | solution.py:347
  213.0 18.9 %collective-permute-start.4 = (f32[3,16,8,128]{3,2,1,0:T(8,128)}, f32[3,16,8,128]{3,2,1,0:T(8,128)S(1)}, u32[]{:S(2)}, u32[]{:S(2)}) collective-permute-start(f32[3,16,8,128]{3,2,1,0:T(8,128)} %get-tuple-element.160), channel_id=1, source_target_pairs={{8,0},{16,8},{24,16},{9,1},{17,9},{25,17},{10,2},{18,10},{26,18},{... | collective-permute-start | bytes 589832 | tf_op jit(solution)/shard_map/ppermute | solution.py:348
  215.3 14.0 %collective-permute-start.5 = (f32[3,8,8,128]{3,2,1,0:T(8,128)}, f32[3,8,8,128]{3,2,1,0:T(8,128)S(1)}, u32[]{:S(2)}, u32[]{:S(2)}) collective-permute-start(f32[3,8,8,128]{3,2,1,0:T(8,128)} %get-tuple-element.162), channel_id=1, source_target_pairs={{1,0},{2,1},{3,2},{4,3},{5,4},{6,5},{7,6},{0,7},{9,8},{10,9},{11,1... | collective-permute-start | bytes 294920 | tf_op jit(solution)/shard_map/ppermute | solution.py:350
  224.0 70.6 %collective-permute-start.7 = (f32[3,8,8,128]{3,2,1,0:T(8,128)}, f32[3,8,8,128]{3,2,1,0:T(8,128)S(1)}, u32[]{:S(2)}, u32[]{:S(2)}) collective-permute-start(f32[3,8,8,128]{3,2,1,0:T(8,128)} %get-tuple-element.161), channel_id=1, source_target_pairs={{0,1},{1,2},{2,3},{3,4},{4,5},{5,6},{6,7},{7,0},{8,9},{9,10},{10,1... | collective-permute-start | bytes 294920 | tf_op jit(solution)/shard_map/ppermute | solution.py:349
  224.0 71.9 %collective-permute-start.6 = (f32[3,16,8,128]{3,2,1,0:T(8,128)}, f32[3,16,8,128]{3,2,1,0:T(8,128)S(1)}, u32[]{:S(2)}, u32[]{:S(2)}) collective-permute-start(f32[3,16,8,128]{3,2,1,0:T(8,128)} %get-tuple-element.159), channel_id=1, source_target_pairs={{0,8},{8,16},{16,24},{1,9},{9,17},{17,25},{2,10},{10,18},{18,26},{... | collective-permute-start | bytes 589832 | tf_op jit(solution)/shard_map/ppermute | solution.py:347
  230.3 64.3 %copy-start.22 = (f32[3,8,8,128]{3,2,1,0:T(8,128)S(1)}, f32[3,8,8,128]{3,2,1,0:T(8,128)}, u32[]{:S(2)}) copy-start(f32[3,8,8,128]{3,2,1,0:T(8,128)} %get-tuple-element.162) | copy-start | bytes 294916
  231.9 63.3 %copy-start.4 = (f32[2,8,8,128]{3,2,1,0:T(8,128)S(1)}, f32[2,8,8,128]{3,2,1,0:T(8,128)}, u32[]{:S(2)}) copy-start(f32[2,8,8,128]{3,2,1,0:T(8,128)} %copy-done.2) | copy-start | bytes 196612
  231.9 63.3 %copy-start.12 = (f32[3,16,8,128]{3,2,1,0:T(8,128)S(1)}, f32[3,16,8,128]{3,2,1,0:T(8,128)}, u32[]{:S(2)}) copy-start(f32[3,16,8,128]{3,2,1,0:T(8,128)} %get-tuple-element.160) | copy-start | bytes 589828
  231.9 63.3 %copy-start.20 = (f32[16,8,128]{2,1,0:T(8,128)S(1)}, f32[16,8,128]{2,1,0:T(8,128)}, u32[]{:S(2)}) copy-start(f32[16,8,128]{2,1,0:T(8,128)} %fusion.16.contact) | copy-start | bytes 196612
  319.1 16.6 %collective-permute-start.8 = (f32[3,16,8,128]{3,2,1,0:T(8,128)}, f32[3,16,8,128]{3,2,1,0:T(8,128)S(1)}, u32[]{:S(2)}, u32[]{:S(2)}) collective-permute-start(f32[3,16,8,128]{3,2,1,0:T(8,128)} %get-tuple-element.164), channel_id=1, source_target_pairs={{8,0},{16,8},{24,16},{9,1},{17,9},{25,17},{10,2},{18,10},{26,18},{... | collective-permute-start | bytes 589832 | tf_op jit(solution)/shard_map/ppermute | solution.py:348
  322.9 10.4 %collective-permute-start.9 = (f32[3,8,8,128]{3,2,1,0:T(8,128)}, f32[3,8,8,128]{3,2,1,0:T(8,128)S(1)}, u32[]{:S(2)}, u32[]{:S(2)}) collective-permute-start(f32[3,8,8,128]{3,2,1,0:T(8,128)} %get-tuple-element.166), channel_id=1, source_target_pairs={{1,0},{2,1},{3,2},{4,3},{5,4},{6,5},{7,6},{0,7},{9,8},{10,9},{11,1... | collective-permute-start | bytes 294920 | tf_op jit(solution)/shard_map/ppermute | solution.py:350
  329.0 67.4 %collective-permute-start.11 = (f32[3,8,8,128]{3,2,1,0:T(8,128)}, f32[3,8,8,128]{3,2,1,0:T(8,128)}, u32[]{:S(2)}, u32[]{:S(2)}) collective-permute-start(f32[3,8,8,128]{3,2,1,0:T(8,128)} %get-tuple-element.165), channel_id=1, source_target_pairs={{0,1},{1,2},{2,3},{3,4},{4,5},{5,6},{6,7},{7,0},{8,9},{9,10},{10,1... | collective-permute-start | bytes 294920 | tf_op jit(solution)/shard_map/ppermute | solution.py:349
  329.0 69.7 %collective-permute-start.10 = (f32[3,16,8,128]{3,2,1,0:T(8,128)}, f32[3,16,8,128]{3,2,1,0:T(8,128)S(1)}, u32[]{:S(2)}, u32[]{:S(2)}) collective-permute-start(f32[3,16,8,128]{3,2,1,0:T(8,128)} %get-tuple-element.163), channel_id=1, source_target_pairs={{0,8},{8,16},{16,24},{1,9},{9,17},{17,25},{2,10},{10,18},{18,26},{... | collective-permute-start | bytes 589832 | tf_op jit(solution)/shard_map/ppermute | solution.py:347
  337.0 60.9 %copy-start.5 = (f32[2,8,8,128]{3,2,1,0:T(8,128)S(1)}, f32[2,8,8,128]{3,2,1,0:T(8,128)}, u32[]{:S(2)}) copy-start(f32[2,8,8,128]{3,2,1,0:T(8,128)} %copy-done.2) | copy-start | bytes 196612
  337.1 60.9 %copy-start.19 = (f32[3,16,8,128]{3,2,1,0:T(8,128)S(1)}, f32[3,16,8,128]{3,2,1,0:T(8,128)}, u32[]{:S(2)}) copy-start(f32[3,16,8,128]{3,2,1,0:T(8,128)} %get-tuple-element.164) | copy-start | bytes 589828
  (21 other events, 647.4 us)
where the time goes:
time: 477 us; the launch traced here: 475 us
  blocking collectives  202 us (42%)
  Pallas kernels  115 us (24%)
  other arithmetic  68.4 us (14%)
  between operations  36.4 us (8%)
  local copies, waits for them, and re-layouts  26.2 us (5%)
  starting transfers between devices  24.6 us (5%)
    unnamed x5, blocking collectives  202 us
    pallas_call x3, Pallas kernels, shards(): f = later_call(weights, q, *direction, mask)  67.1 us
    pallas_call x1, Pallas kernels, shards(): outs = first_call(load, mod, *multipliers, mask)  47.6 us
    add x18, other arithmetic, axpy(): return tuple((x + s * y for x, y in zip(a, b)))  13.4 us
    ppermute x3, starting transfers between devices, jumps(): from_right = lax.ppermute(first_y, 'surf', back(ring))  11.8 us
  transfers between devices with their start and end apart: 12, of which 0 were waited for; matrix products, arithmetic and copies ran while one was open for 12% of the time, Pallas kernels for 0%

commit v1 on v0

v1 whole, which is shorter than its diff:
```python
import functools

import jax
import jax.numpy as jnp
import numpy as np
from jax import lax
from jax.experimental import pallas as pl
from jax.experimental.pallas import tpu as pltpu
from jax.sharding import PartitionSpec as P

ITERS = 3
SWEEPS = 6
COUPLING_SCALE = (0.0, 1.0, 0.5, 0.25)
RELAXATION = 0.6
PLANE = [(dx, dy) for dx in (-1, 0, 1) for dy in (-1, 0, 1)]
SAME = [o for o in PLANE if o != (0, 0)]
SUB, LANE = 8, 128


def shift_up(t):
    lane = lax.broadcasted_iota(jnp.int32, t.shape, 1)
    r = pltpu.roll(t, 1, 1)
    return jnp.where(lane == 0, pltpu.roll(r, 1, 0), r)


def shift_down(t):
    lane = lax.broadcasted_iota(jnp.int32, t.shape, 1)
    r = pltpu.roll(t, LANE - 1, 1)
    return jnp.where(lane == LANE - 1, pltpu.roll(r, SUB - 1, 0), r)


def setup_weights(nx, ny, mod_ref, mp, w_ref, q_ref):
    zero = jnp.zeros((SUB, LANE), jnp.float32)

    def clear(y, c):
        mp[0, y] = zero
        mp[nx + 1, y] = zero
        return c

    lax.fori_loop(0, ny + 2, clear, 0)

    def fill(x, c):
        mp[x + 1, 0] = zero
        mp[x + 1, ny + 1] = zero
        mp[x + 1, pl.ds(1, ny)] = mod_ref[x]
        return c

    lax.fori_loop(0, nx, fill, 0)
    sub = lax.broadcasted_iota(jnp.int32, (SUB, LANE), 0)
    lane = lax.broadcasted_iota(jnp.int32, (SUB, LANE), 1)
    first = (sub == 0) & (lane == 0)
    last = (sub == SUB - 1) & (lane == LANE - 1)

    def column(i, c):
        x = i // ny
        y = i % ny
        a = mp[x + 1, y + 1]
        up = jnp.where(first, 0.0, shift_up(a))
        down = jnp.where(last, 0.0, shift_down(a))
        total0 = zero
        total_p = zero
        total_m = zero
        for dx, dy in PLANE:
            b = mp[x + 1 + dx, y + 1 + dy]
            k = abs(dx) + abs(dy)
            if k:
                w = (2.0 * COUPLING_SCALE[k]) * a * b / (a + b)
                w_ref[SAME.index((dx, dy)), x, y] = w
                total0 = total0 + w
            scale = 2.0 * COUPLING_SCALE[k + 1]
            j = PLANE.index((dx, dy))
            w = scale * up * b / jnp.maximum(up + b, 1e-30)
            w_ref[8 + j, x, y] = w
            total_p = total_p + w
            w = scale * down * b / jnp.maximum(down + b, 1e-30)
            w_ref[17 + j, x, y] = w
            total_m = total_m + w
        diag = total0 + shift_down(total_p) + shift_up(total_m)
        q_ref[x, y] = RELAXATION / diag
        return c

    lax.fori_loop(0, nx * ny, column, 0)


def column_update(x, y, src, dst, s_ref, w_ref, q_ref):
    center, plus, minus, mid = [], [], [], []
    for comp in range(3):
        mid.append(s_ref[comp, x, y])
    for n, (dx, dy) in enumerate(PLANE):
        wp = w_ref[8 + n, x, y]
        wm = w_ref[17 + n, x, y]
        w0 = w_ref[SAME.index((dx, dy)), x, y] if (dx, dy) != (0, 0) else None
        for comp in range(3):
            v = src[comp, x + 1 + dx, y + 1 + dy]
            if n == 0:
                plus.append(wp * v)
                minus.append(wm * v)
            else:
                plus[comp] = plus[comp] + wp * v
                minus[comp] = minus[comp] + wm * v
            if w0 is None:
                center.append(v)
            else:
                mid[comp] = mid[comp] + w0 * v
    q = q_ref[x, y]
    for comp in range(3):
        total = mid[comp] + shift_down(plus[comp]) + shift_up(minus[comp])
        dst[comp, x + 1, y + 1] = (1.0 - RELAXATION) * center[comp] + q * total


def sweep(nx, ny, depth, src, dst, s_ref, w_ref, q_ref):
    full = min(nx, 2 * (depth + 1))
    step = 4

    def rows(i, c):
        r = i // (ny // step)
        y0 = (i % (ny // step)) * step
        x = r if full == nx else jnp.where(r <= depth, r, r + (nx - full))
        for j in range(step):
            column_update(x, y0 + j, src, dst, s_ref, w_ref, q_ref)
        return c

    lax.fori_loop(0, full * (ny // step), rows, 0)
    if full < nx:
        def sides(i, c):
            x = depth + 1 + i
            for j in range(depth + 1):
                column_update(x, j, src, dst, s_ref, w_ref, q_ref)
                column_update(x, ny - 1 - j, src, dst, s_ref, w_ref, q_ref)
            return c

        lax.fori_loop(0, nx - full, sides, 0)


def relax(nx, ny, local, va, vb, s_ref, w_ref, q_ref):
    deepest = (min(nx, ny) - 1) // 2

    def start(x, c):
        for comp in range(3):
            va[comp, x + 1, pl.ds(1, ny)] = q_ref[x] * s_ref[comp, x]
            if local:
                vb[comp, x + 1, pl.ds(1, ny)] = jnp.zeros((ny, SUB, LANE), jnp.float32)
        return c

    lax.fori_loop(0, nx, start, 0)
    bufs = (va, vb)
    for k in range(1, SWEEPS):
        depth = min(deepest, SWEEPS - 1 - k)
        if local:
            depth = min(depth, k)
        sweep(nx, ny, depth, bufs[(k - 1) % 2], bufs[k % 2], s_ref, w_ref, q_ref)
    return bufs[(SWEEPS - 1) % 2]


def clear_halo(nx, ny, va, vb):
    zero = jnp.zeros((SUB, LANE), jnp.float32)
    for v in (va, vb):
        for comp in range(3):
            v[comp, 0] = jnp.zeros((ny + 2, SUB, LANE), jnp.float32)
            v[comp, nx + 1] = jnp.zeros((ny + 2, SUB, LANE), jnp.float32)

            def side(x, c):
                v[comp, x + 1, 0] = zero
                v[comp, x + 1, ny + 1] = zero
                return c

            lax.fori_loop(0, nx, side, 0)


def add_faces(nx, ny, s_ref, own_x, up_x, own_y, left_y, contact, mask, sign):
    for comp in range(3):
        s_ref[comp, nx - 1] = s_ref[comp, nx - 1] + sign * own_x[comp]
        s_ref[comp, 0] = s_ref[comp, 0] - sign * up_x[comp]

        def side(x, c):
            s_ref[comp, x, ny - 1] = s_ref[comp, x, ny - 1] + sign * own_y[comp, x]
            s_ref[comp, x, 0] = s_ref[comp, x, 0] - sign * left_y[comp, x]
            return c

        lax.fori_loop(0, nx, side, 0)
    s_ref[0, 0] = s_ref[0, 0] - sign * contact[...] * mask[...]


def coarse_constants(n_depth, n_across, face_x, face_y):
    path = 2.0 * np.eye(n_depth) - np.eye(n_depth, k=1) - np.eye(n_depth, k=-1)
    path[0, 0] = 1.0
    eye = np.eye(n_across)
    cycle = 2.0 * eye - np.roll(eye, 1, axis=1) - np.roll(eye, -1, axis=1)
    base = face_x * np.kron(path, eye) + face_y * np.kron(np.eye(n_depth), cycle)
    part_x = np.kron(np.eye(n_depth) - np.eye(n_depth, k=-1), eye)
    part_y = np.kron(np.eye(n_depth), eye - np.roll(eye, 1, axis=0))
    return np.stack([part_x, part_y, part_x.T, part_y.T, np.linalg.inv(base)])


def dot(a, b):
    return jnp.dot(a, b, precision=lax.Precision.HIGHEST, preferred_element_type=jnp.float32)


def one(value):
    return jnp.sum(jnp.sum(value, axis=0, keepdims=True), axis=1, keepdims=True)


def whole(value):
    return one(jnp.sum(value.reshape((-1, SUB, LANE)), axis=0))


def feti_kernel(nx, ny, nz, n_depth, n_across, load, mod, mask, maps,
                mult_x, mult_y, mult_c, mp, va, vb, s_ref, w_ref, q_ref,
                res_x, res_y, res_c, dir_x, dir_y, dir_c, im_x, im_y, im_c, up_x, up_y,
                below_in, above_in, right_in, left_in, sent, table,
                face_send, face_recv, row_send, row_recv):
    f32 = jnp.float32
    total = n_depth * n_across
    body = lax.axis_index("body")
    surf = lax.axis_index("surf")
    me = body * n_across + surf
    below = lax.rem(body + 1, n_depth)
    above = lax.rem(body + n_depth - 1, n_depth)
    right = lax.rem(surf + 1, n_across)
    left = lax.rem(surf + n_across - 1, n_across)
    mesh_id = pl.DeviceIdType.MESH
    inner = jnp.where(body > 0, 1.0, 0.0).astype(f32)
    outer = jnp.where(body < n_depth - 1, 1.0, 0.0).astype(f32)
    area_x, area_y = float(ny * nz), float(nx * nz)
    lane = lax.broadcasted_iota(jnp.int32, (SUB, LANE), 1)
    rows = lax.broadcasted_iota(jnp.int32, (total, LANE), 0)
    lanes = lax.broadcasted_iota(jnp.int32, (total, LANE), 1)

    barrier = pltpu.get_barrier_semaphore()

    def greet(k, c):
        peer = lax.rem(me + k, total)
        pl.semaphore_signal(barrier, inc=1, device_id=(peer // n_across, lax.rem(peer, n_across)),
                            device_id_type=mesh_id)
        return c

    lax.fori_loop(1, total, greet, 0)

    def row_copy(slot, k, peer, owner):
        return pltpu.make_async_remote_copy(
            src_ref=sent.at[slot], dst_ref=table.at[slot, owner],
            send_sem=row_send.at[slot, k], recv_sem=row_recv.at[slot, owner],
            device_id=(peer // n_across, lax.rem(peer, n_across)), device_id_type=mesh_id)

    def post(slot, values):
        row = jnp.zeros((SUB, LANE), f32)
        for k, value in enumerate(values):
            row = jnp.where(lane == k, value, row)
        sent[slot] = row
        table[slot, me] = row

        def send(k, c):
            row_copy(slot, k, lax.rem(me + k, total), me).start()
            return c

        lax.fori_loop(1, total, send, 0)

    def collect(slot):
        def wait(k, c):
            peer = lax.rem(me + k, total)
            row_copy(slot, k, peer, peer).wait()
            return c

        lax.fori_loop(1, total, wait, 0)
        return table[slot, :, 0, :]

    def face_copies():
        pairs = (
            (vb.at[:, 1, pl.ds(1, ny)], below_in, (above, surf)),
            (vb.at[:, nx, pl.ds(1, ny)], above_in, (below, surf)),
            (vb.at[:, pl.ds(1, nx), 1], right_in, (body, left)),
            (vb.at[:, pl.ds(1, nx), ny], left_in, (body, right)),
        )
        return [pltpu.make_async_remote_copy(
            src_ref=a, dst_ref=b, send_sem=face_send.at[i], recv_sem=face_recv.at[i],
            device_id=peer, device_id_type=mesh_id) for i, (a, b, peer) in enumerate(pairs)]

    def at(value, row, column):
        return one(jnp.where((rows == row) & (lanes == column), value, 0.0))

    def jumps(sign):
        copies = face_copies()
        for copy in copies:
            copy.start()
        for copy in copies:
            copy.wait()
        for comp in range(3):
            first = vb[comp, 1, pl.ds(1, ny)]
            im_x[comp] = sign * (vb[comp, nx, pl.ds(1, ny)] - outer * below_in[comp])
            up_x[comp] = sign * (inner * (above_in[comp] - first))
            im_y[comp] = sign * (vb[comp, pl.ds(1, nx), ny] - right_in[comp])
            up_y[comp] = sign * (left_in[comp] - vb[comp, pl.ds(1, nx), 1])
        im_c[...] = (-sign) * vb[0, 1, pl.ds(1, ny)] * mask[...]

    own_count = whole(mask[...])

    def statistics():
        sums = [whole(im_x[comp]) for comp in range(3)] + [whole(im_y[comp]) for comp in range(3)]
        sums.append(whole(im_c[...]))
        square = jnp.zeros((SUB, LANE), f32)
        for comp in range(3):
            cx = im_x[comp] - sums[comp] / area_x
            cy = im_y[comp] - sums[3 + comp] / area_y
            square = square + jnp.sum(cx * cx, axis=0) + jnp.sum(cy * cy, axis=0)
        cc = im_c[...] - (sums[6] / jnp.maximum(own_count, 1.0)) * mask[...]
        square = square + jnp.sum(cc * cc, axis=0)
        return sums + [one(square)]

    def own_dot(a_x, a_y, a_c):
        acc = jnp.sum(a_c[...] * im_c[...], axis=0)
        for comp in range(3):
            acc = acc + jnp.sum(a_x[comp, 0] * im_x[comp], axis=0)
            acc = acc + jnp.sum(a_y[comp, 0] * im_y[comp], axis=0)
        return one(acc)

    load_sums = [whole(jnp.sum(load[comp], axis=0)) for comp in range(3)]
    pl.semaphore_wait(barrier, total - 1)
    post(0, load_sums + [own_count])
    setup_weights(nx, ny, mod, mp, w_ref, q_ref)
    clear_halo(nx, ny, va, vb)
    s_ref[...] = load[...]
    begin = collect(0)
    counts = begin[:, 3:4]

    corner = maps[4, 0:n_across, 0:n_across]
    count_face = counts[0:n_across]
    sq_row = lax.broadcasted_iota(jnp.int32, (n_across, n_across), 0)
    sq_col = lax.broadcasted_iota(jnp.int32, (n_across, n_across), 1)
    work = jnp.where(sq_row == sq_col, 1.0, 0.0) + count_face * corner
    other = jnp.where(sq_row == sq_col, count_face, 0.0)
    row_id = lax.broadcasted_iota(jnp.int32, (n_across, 1), 0)
    for k in range(n_across):
        scale = 1.0 / work[k : k + 1, k : k + 1]
        pivot, tail = work[k : k + 1] * scale, other[k : k + 1] * scale
        factor = work[:, k : k + 1]
        work = jnp.where(row_id == k, pivot, work - factor * pivot)
        other = jnp.where(row_id == k, tail, other - factor * tail)

    def coarse_solve(rhs):
        tangent = dot(maps[4], rhs)
        small = jnp.zeros((n_across, LANE), f32)
        for k in range(n_across):
            small = small + other[:, k : k + 1] * tangent[k : k + 1]
        fix = jnp.zeros((total, LANE), f32)
        for k in range(n_across):
            fix = fix + maps[4, :, k : k + 1] * small[k : k + 1]
        return jnp.where(lanes == 0, tangent - fix, tangent)

    def lifted(alpha):
        along_x = dot(maps[2], alpha)
        along_y = dot(maps[3], alpha)
        own = [[at(along_x, me, c) for c in range(3)],
               [inner * at(along_x, above * n_across + surf, c) for c in range(3)],
               [at(along_y, me, c) for c in range(3)],
               [at(along_y, body * n_across + left, c) for c in range(3)],
               at(alpha, me, 0)]
        return along_x, along_y, own

    def project(tab):
        by_x = dot(maps[0], tab)
        by_y = dot(maps[1], tab)
        rhs = by_x + pltpu.roll(by_y, LANE - 3, 1)
        rhs = rhs - jnp.where(lanes == 0, pltpu.roll(tab, LANE - 6, 1), 0.0)
        alpha = coarse_solve(jnp.where(lanes < 3, rhs, 0.0))
        along_x, along_y, own = lifted(alpha)
        ex = jnp.where(lanes < 3, tab / area_x - along_x, 0.0)
        ey = jnp.where(lanes < 3, pltpu.roll(tab, LANE - 3, 1) / area_y - along_y, 0.0)
        ec = tab[:, 6:7] / jnp.maximum(counts, 1.0) + alpha[:, 0:1]
        norm = one(jnp.where(lanes == 7, tab, 0.0) + area_x * ex * ex + area_y * ey * ey
                   + jnp.where(lanes == 0, counts * ec * ec, 0.0))
        for comp in range(3):
            im_x[comp] = im_x[comp] - own[0][comp]
            up_x[comp] = up_x[comp] - own[1][comp]
            im_y[comp] = im_y[comp] - own[2][comp]
            up_y[comp] = up_y[comp] - own[3][comp]
        im_c[...] = im_c[...] + own[4] * mask[...]
        return norm

    own = lifted(coarse_solve(jnp.where(lanes < 3, begin, 0.0)))[2]
    for comp in range(3):
        dir_x[comp, 0] = jnp.broadcast_to(own[0][comp], (ny, SUB, LANE))
        dir_x[comp, 1] = jnp.broadcast_to(own[1][comp], (ny, SUB, LANE))
        dir_y[comp, 0] = jnp.broadcast_to(own[2][comp], (nx, SUB, LANE))
        dir_y[comp, 1] = jnp.broadcast_to(own[3][comp], (nx, SUB, LANE))
        mult_x[comp] = dir_x[comp, 0]
        mult_y[comp] = dir_y[comp, 0]
    dir_c[...] = -own[4] * mask[...]
    mult_c[...] = dir_c[...]

    def put_faces(sign):
        add_faces(nx, ny, s_ref, dir_x.at[:, 0], dir_x.at[:, 1], dir_y.at[:, 0], dir_y.at[:, 1],
                  dir_c, mask, sign)

    put_faces(-1.0)
    relax(nx, ny, False, va, vb, s_ref, w_ref, q_ref)
    jumps(-1.0)
    post(1, statistics())
    rr = project(collect(1))
    for comp in range(3):
        for k, (a, b) in enumerate(((im_x, im_y), (up_x, up_y))):
            res_x[comp, k] = a[comp]
            dir_x[comp, k] = a[comp]
            res_y[comp, k] = b[comp]
            dir_y[comp, k] = b[comp]
    res_c[...] = im_c[...]
    dir_c[...] = im_c[...]

    def climb(step):
        for comp in range(3):
            mult_x[comp] = mult_x[comp] + step * dir_x[comp, 0]
            mult_y[comp] = mult_y[comp] + step * dir_y[comp, 0]
        mult_c[...] = mult_c[...] + step * dir_c[...]

    for iteration in range(ITERS):
        slot = iteration % 2
        s_ref[...] = jnp.zeros_like(s_ref)
        put_faces(1.0)
        relax(nx, ny, True, va, vb, s_ref, w_ref, q_ref)
        if iteration + 1 == ITERS:
            acc = -jnp.sum(dir_c[...] * vb[0, 1, pl.ds(1, ny)] * mask[...], axis=0)
            for comp in range(3):
                acc = acc + jnp.sum(dir_x[comp, 0] * vb[comp, nx, pl.ds(1, ny)], axis=0)
                acc = acc - jnp.sum(dir_x[comp, 1] * vb[comp, 1, pl.ds(1, ny)], axis=0)
                acc = acc + jnp.sum(dir_y[comp, 0] * vb[comp, pl.ds(1, nx), ny], axis=0)
                acc = acc - jnp.sum(dir_y[comp, 1] * vb[comp, pl.ds(1, nx), 1], axis=0)
            post(slot, [one(acc)])
            bottom = one(jnp.where(lanes == 0, collect(slot), 0.0))
            climb(rr / bottom)
            break
        jumps(1.0)
        post(slot, statistics() + [own_dot(dir_x, dir_y, dir_c), own_dot(res_x, res_y, res_c)])
        tab = collect(slot)
        norm = project(tab)
        step = rr / one(jnp.where(lanes == 8, tab, 0.0))
        cross = one(jnp.where(lanes == 9, tab, 0.0))
        new = rr + 2.0 * step * cross + step * step * norm
        climb(step)
        beta = new / rr
        for comp in range(3):
            for k, (a, b) in enumerate(((im_x, im_y), (up_x, up_y))):
                value = res_x[comp, k] + step * a[comp]
                res_x[comp, k] = value
                dir_x[comp, k] = value + beta * dir_x[comp, k]
                value = res_y[comp, k] + step * b[comp]
                res_y[comp, k] = value
                dir_y[comp, k] = value + beta * dir_y[comp, k]
        value = res_c[...] + step * im_c[...]
        res_c[...] = value
        dir_c[...] = value + beta * dir_c[...]
        rr = new


def shards(external_load, modulus, active):
    nx, ny, nz = modulus.shape
    n_depth = lax.axis_size("body")
    n_across = lax.axis_size("surf")
    total = n_depth * n_across
    f32 = jnp.float32
    top = (lax.axis_index("body") == 0).astype(f32)
    mask = (active.astype(f32) * top).reshape(ny, SUB, LANE)
    maps = jnp.asarray(coarse_constants(n_depth, n_across, float(ny * nz), float(nx * nz)), f32)
    spec = pl.BlockSpec(memory_space=pltpu.VMEM)
    face_x, face_y, tiles = (3, ny, SUB, LANE), (3, nx, SUB, LANE), (ny, SUB, LANE)
    two_x, two_y = (3, 2, ny, SUB, LANE), (3, 2, nx, SUB, LANE)
    iterate = (3, nx + 2, ny + 2, SUB, LANE)
    shapes = [(nx + 2, ny + 2, SUB, LANE), iterate, iterate, (3, nx, ny, SUB, LANE),
              (26, nx, ny, SUB, LANE), (nx, ny, SUB, LANE),
              two_x, two_y, tiles, two_x, two_y, tiles, face_x, face_y, tiles, face_x, face_y,
              face_x, face_x, face_y, face_y, (2, SUB, LANE), (2, total, SUB, LANE)]
    out = pl.pallas_call(
        functools.partial(feti_kernel, nx, ny, nz, n_depth, n_across),
        out_shape=tuple(jax.ShapeDtypeStruct(s, f32) for s in (face_x, face_y, tiles)),
        in_specs=[spec] * 4, out_specs=(spec,) * 3,
        scratch_shapes=[pltpu.VMEM(s, f32) for s in shapes] + [
            pltpu.SemaphoreType.DMA((4,)), pltpu.SemaphoreType.DMA((4,)),
            pltpu.SemaphoreType.DMA((2, total)), pltpu.SemaphoreType.DMA((2, total))],
        compiler_params=pltpu.CompilerParams(
            vmem_limit_bytes=56 * 1024 * 1024, collective_id=0, has_side_effects=True),
    )(external_load.reshape(3, nx, ny, SUB, LANE), modulus.reshape(nx, ny, SUB, LANE), mask, maps)
    return (out[0].reshape(3, 1, ny, nz), out[1].reshape(3, nx, 1, nz), out[2].reshape(1, ny, nz))


def solution(mesh):
    placed = (P(None, "body", "surf", None), P("body", "surf", None), P("surf", None))
    return jax.shard_map(
        shards,
        mesh=mesh,
        in_specs=placed,
        out_specs=(
            P(None, "body", "surf", None),
            P(None, "body", "surf", None),
            P("body", "surf", None),
        ),
        check_vma=False,
    )
```

time: 477 us -> 156 us (0.33)
  blocking collectives: 202 us -> 0 us
  other arithmetic: 68.4 us -> 0.85 us
  between operations: 36.4 us -> 0.65 us
  Pallas kernels: 115 us -> 144 us
  starting transfers between devices: 24.6 us -> 0 us
  local copies, waits for them, and re-layouts: 26.2 us -> 10.1 us
    unnamed x5 -> x0, blocking collectives: 202 us -> none
    reduce_sum x30 -> x0, other arithmetic: 31.3 us -> none  [the longest x6 5.36 us: own_dot(): return jnp.sum(a[0] * b[0]) + jnp.sum(a[2] * b[2]) + jnp.sum(a[4] * b[4])]
    pallas_call x4 -> x1, Pallas kernels: 115 us -> 144 us  [shards(): pl.pallas_call(functools.partial(feti_kernel, nx, ny, nz, n_depth, n_acro...]
    ppermute x12 -> x0, starting transfers between devices: 24.6 us -> none  [the longest x3 11.8 us: jumps(): from_right = lax.ppermute(first_y, 'surf', back(ring))]
    add x19 -> x0, other arithmetic: 13.5 us -> none  [the longest x18 13.4 us: axpy(): return tuple((x + s * y for x, y in zip(a, b)))]
    slice x51 -> x0, local copies, waits for them, and re-layouts: 13.2 us -> none  [the longest x8 4.62 us: shards(): pivot = work[k] / work[k, k]]
    mul x12 -> x0, other arithmetic: 6.52 us -> none  [the longest x8 5.21 us: shards(): work = (work - work[:, k:k + 1] * pivot[None]).at[k].set(pivot)]
    div x12 -> x0, other arithmetic: 5.21 us -> none  [the longest x8 5.19 us: shards(): pivot = work[k] / work[k, k]]
  transfers between devices with their start and end apart: 12 -> 0, of which waited for: 0 -> 0; matrix products, arithmetic and copies ran while one was open for 12% -> 0% of each run, Pallas kernels for 0% -> 0%
where the time goes in v1:
time: 156 us
  Pallas kernels  144 us (92%)
  local copies, waits for them, and re-layouts  10.1 us (6%)
    pallas_call x1, Pallas kernels, shards(): pl.pallas_call(functools.partial(feti_kernel, nx, ny, nz, n_depth, n_acro...  144 us
    unnamed x4, local copies, waits for them, and re-layouts  7.02 us

profile of v1, /device:TPU:0, one launch (start us, length us, event | category | flops | bytes accessed | tf_op | source)
XLA Modules:
  0.0 156.1 jit_solution(13075369138534358386)
XLA Ops:
  0.6 0.8 multiply_bitcast_fusion
  1.5 0.6 copy.11
  2.1 1.9 %copy.10 = f32[16,8,8,128]{3,2,1,0:T(8,128)} copy(f32[16,8,8,128]{3,1,2,0:T(8,128)} %bitcast.19) | data formatting | bytes 1048576
  4.1 2.9 %copy.9 = f32[48,8,8,128]{3,2,1,0:T(8,128)} copy(f32[48,8,8,128]{3,1,2,0:T(8,128)} %bitcast.18) | data formatting | bytes 3145728
  7.0 144.4 %shard_map.67 = (f32[3,16,8,128]{3,2,1,0:T(8,128)}, f32[3,8,8,128]{3,2,1,0:T(8,128)}, f32[16,8,128]{2,1,0:T(8,128)}) custom-call(f32[3,8,16,8,128]{4,3,2,1,0:T(8,128)} %bitcast.16, f32[8,16,8,128]{3,2,1,0:T(8,128)} %bitcast.17, f32[16,8,128]{2,1,0:T(8,128)} %bitcast.20, f32[5,32,32]{2,1,0:T(8,128)} %constant.9.clone.maps), custom_call_target="tpu_custom_call" | custom-call | tf_op jit(solution)/shard_map/pallas_call | solution.py:470
  151.4 1.6 %reshape.27 = f32[3,1,16,1024]{3,2,0,1:T(8,128)} reshape(f32[3,16,8,128]{3,2,1,0:T(8,128)} %get-tuple-element.6) | data formatting | bytes 393216 | tf_op jit(solution)/shard_map/reshape | solution.py:480
  153.0 1.5 reshape.29
  154.5 1.5 copy.13

commit v2 on v1

--- a/solution.py
+++ b/solution.py
@@ -51,9 +51,7 @@
     first = (sub == 0) & (lane == 0)
     last = (sub == SUB - 1) & (lane == LANE - 1)
 
-    def column(i, c):
-        x = i // ny
-        y = i % ny
+    def column(x, y):
         a = mp[x + 1, y + 1]
         up = jnp.where(first, 0.0, shift_up(a))
         down = jnp.where(last, 0.0, shift_down(a))
@@ -77,9 +75,16 @@
             total_m = total_m + w
         diag = total0 + shift_down(total_p) + shift_up(total_m)
         q_ref[x, y] = RELAXATION / diag
+
+    batch = 8
+
+    def columns(i, c):
+        per_row = ny // batch
+        for j in range(batch):
+            column(i // per_row, lax.rem(i, per_row) * batch + j)
         return c
 
-    lax.fori_loop(0, nx * ny, column, 0)
+    lax.fori_loop(0, nx * ny // batch, columns, 0)
 
 
 def column_update(x, y, src, dst, s_ref, w_ref, q_ref):
@@ -110,7 +115,7 @@
 
 def sweep(nx, ny, depth, src, dst, s_ref, w_ref, q_ref):
     full = min(nx, 2 * (depth + 1))
-    step = 4
+    step = 8
 
     def rows(i, c):
         r = i // (ny // step)
@@ -122,14 +127,17 @@
 
     lax.fori_loop(0, full * (ny // step), rows, 0)
     if full < nx:
+        batch = max(b for b in (1, 2, 3) if (nx - full) % b == 0 and b * (depth + 1) <= 4 or b == 1)
+
         def sides(i, c):
-            x = depth + 1 + i
-            for j in range(depth + 1):
-                column_update(x, j, src, dst, s_ref, w_ref, q_ref)
-                column_update(x, ny - 1 - j, src, dst, s_ref, w_ref, q_ref)
+            for k in range(batch):
+                x = depth + 1 + i * batch + k
+                for j in range(depth + 1):
+                    column_update(x, j, src, dst, s_ref, w_ref, q_ref)
+                    column_update(x, ny - 1 - j, src, dst, s_ref, w_ref, q_ref)
             return c
 
-        lax.fori_loop(0, nx - full, sides, 0)
+        lax.fori_loop(0, (nx - full) // batch, sides, 0)
 
 
 def relax(nx, ny, local, va, vb, s_ref, w_ref, q_ref):
@@ -228,19 +236,28 @@
 
     barrier = pltpu.get_barrier_semaphore()
 
-    def greet(k, c):
-        peer = lax.rem(me + k, total)
-        pl.semaphore_signal(barrier, inc=1, device_id=(peer // n_across, lax.rem(peer, n_across)),
-                            device_id_type=mesh_id)
-        return c
-
-    lax.fori_loop(1, total, greet, 0)
-
-    def row_copy(slot, k, peer, owner):
+    peer_surf = [lax.rem(surf + k, n_across) for k in range(n_across)]
+
+    def every_peer(act):
+        for k in range(1, n_across):
+            act(k, body, peer_surf[k])
+
+        def others(d, c):
+            there = lax.rem(body + d, n_depth)
+            for k in range(n_across):
+                act(d * n_across + k, there, peer_surf[k])
+            return c
+
+        lax.fori_loop(1, n_depth, others, 0)
+
+    every_peer(lambda k, b, s: pl.semaphore_signal(
+        barrier, inc=1, device_id=(b, s), device_id_type=mesh_id))
+
+    def row_copy(slot, k, b, s, owner):
         return pltpu.make_async_remote_copy(
             src_ref=sent.at[slot], dst_ref=table.at[slot, owner],
             send_sem=row_send.at[slot, k], recv_sem=row_recv.at[slot, owner],
-            device_id=(peer // n_across, lax.rem(peer, n_across)), device_id_type=mesh_id)
+            device_id=(b, s), device_id_type=mesh_id)
 
     def post(slot, values):
         row = jnp.zeros((SUB, LANE), f32)
@@ -249,19 +266,10 @@
         sent[slot] = row
         table[slot, me] = row
 
-        def send(k, c):
-            row_copy(slot, k, lax.rem(me + k, total), me).start()
-            return c
-
-        lax.fori_loop(1, total, send, 0)
+        every_peer(lambda k, b, s: row_copy(slot, k, b, s, me).start())
 
     def collect(slot):
-        def wait(k, c):
-            peer = lax.rem(me + k, total)
-            row_copy(slot, k, peer, peer).wait()
-            return c
-
-        lax.fori_loop(1, total, wait, 0)
+        every_peer(lambda k, b, s: row_copy(slot, k, b, s, b * n_across + s).wait())
         return table[slot, :, 0, :]
 
     def face_copies():

time: 156 us -> 124 us (0.79)
  Pallas kernels: 144 us -> 112 us
    pallas_call x1, Pallas kernels: 144 us -> 112 us  [shards(): pl.pallas_call(functools.partial(feti_kernel, nx, ny, nz, n_depth, n_acro...]
where the time goes in v2:
time: 124 us; the launch traced here: 123 us
  Pallas kernels  112 us (90%)
  local copies, waits for them, and re-layouts  10.1 us (8%)
    pallas_call x1, Pallas kernels, shards(): pl.pallas_call(functools.partial(feti_kernel, nx, ny, nz, n_depth, n_acro...  112 us
    unnamed x4, local copies, waits for them, and re-layouts  7.02 us

profile of v2, /device:TPU:0, one launch (start us, length us, event | category | flops | bytes accessed | tf_op | source)
XLA Modules:
  0.0 123.4 jit_solution(14569171709085895575)
XLA Ops:
  0.6 0.8 multiply_bitcast_fusion
  1.5 0.6 copy.11
  2.1 1.9 %copy.10 = f32[16,8,8,128]{3,2,1,0:T(8,128)} copy(f32[16,8,8,128]{3,1,2,0:T(8,128)} %bitcast.19) | data formatting | bytes 1048576
  4.1 2.9 %copy.9 = f32[48,8,8,128]{3,2,1,0:T(8,128)} copy(f32[48,8,8,128]{3,1,2,0:T(8,128)} %bitcast.18) | data formatting | bytes 3145728
  7.0 111.7 %shard_map.67 = (f32[3,16,8,128]{3,2,1,0:T(8,128)}, f32[3,8,8,128]{3,2,1,0:T(8,128)}, f32[16,8,128]{2,1,0:T(8,128)}) custom-call(f32[3,8,16,8,128]{4,3,2,1,0:T(8,128)} %bitcast.16, f32[8,16,8,128]{3,2,1,0:T(8,128)} %bitcast.17, f32[16,8,128]{2,1,0:T(8,128)} %bitcast.20, f32[5,32,32]{2,1,0:T(8,128)} %constant.9.clone.maps), custom_call_target="tpu_custom_call" | custom-call | tf_op jit(solution)/shard_map/pallas_call | solution.py:478
  118.7 1.6 %reshape.27 = f32[3,1,16,1024]{3,2,0,1:T(8,128)} reshape(f32[3,16,8,128]{3,2,1,0:T(8,128)} %get-tuple-element.6) | data formatting | bytes 393216 | tf_op jit(solution)/shard_map/reshape | solution.py:488
  120.3 1.5 %reshape.29 = f32[1,16,1024]{2,1,0:T(8,128)} reshape(f32[16,8,128]{2,1,0:T(8,128)} %get-tuple-element.8) | data formatting | bytes 131072 | tf_op jit(solution)/shard_map/reshape | solution.py:488
  121.8 1.5 %copy.13 = f32[3,8,1,1024]{3,2,1,0:T(1,128)} copy(f32[3,8,1,1024]{3,2,1,0:T(1,128)} %bitcast.22) | data formatting | bytes 196608
